TPU v7x, 768 devices: a whole 4x8x12 slice. The times are simulated.
768 devices in a mesh: dp: 16 (over y, core), section: 48 (over x, z).
Axes of the slice: x: 4, y: 8, z: 12, core: 2. Of those that a mesh axis runs over, the one named last changes fastest.
Arguments:
- lat_raw: bfloat16 [48, 16, 16, 16], P('section', None, 'dp'), may hold values from -6 to 6
- txt_raw: bfloat16 [48, 16, 16, 4096], P('section', None, 'dp'), may hold values from -6 to 6
- lat_embed: bfloat16 [16, 1024], replicated, may hold values from -1.5 to 1.5
- txt_embed: bfloat16 [4096, 1024], replicated, may hold values from -0.09375 to 0.09375
- image_owner: int32 [48, 16], replicated, may hold values from 0 to 15, each once within a row
- text_len: int32 [48, 16], replicated, may hold values from 1 to 16
- weights: bfloat16 [48, 1024, 1024], P('section', 'dp'), may hold values from -0.1875 to 0.1875
- top_grad: bfloat16 [16, 48, 32, 1024], P('dp', 'section'), may hold values from -0.75 to 0.75
Outputs:
- weight_grads: float32 [48, 1024, 1024], P('section', 'dp')
Inputs may be any that keep to these rules, and one draw needn't show every extreme that they name: `image_owner`: each row names every data shard exactly once.
All inputs are finite; a program needn't handle non-finite values.
Results may differ from a plain program's by a relative error of at most 0.023.
Values may be sent and summed in bfloat16 or wider, within the bound.
A program may use at most 32 MiB of HBM per device.

v0:
```python
import jax
import jax.numpy as jnp
from jax import lax
from jax.sharding import PartitionSpec as P

LAT = 16
PIPE = 8


norm_eps = 1e-06


def extended(cells, sides, width):
    for axis, dim in sides:
        count = lax.axis_size(axis)
        ends = count - 1
        head = lax.slice_in_dim(cells, 0, width, axis=dim)
        tail = lax.slice_in_dim(cells, cells.shape[dim] - width, cells.shape[dim], axis=dim)
        cells = jnp.concatenate(
            [
                lax.ppermute(tail, axis, [(i, (i + 1) % count) for i in range(ends)]),
                cells,
                lax.ppermute(head, axis, [((i + 1) % count, i) for i in range(ends)]),
            ],
            axis=dim,
        )
    return cells


def modulate(tokens_in, text_mask, text_count):
    inv_norm = lax.rsqrt(jnp.mean(tokens_in * tokens_in, axis=1, keepdims=True) + norm_eps)
    normed = tokens_in * inv_norm
    pooled = 0.5 * jnp.sum(normed * text_mask[:, None], axis=0) / text_count
    return normed * (1.0 + pooled)[None, :]


def silu_slope(gate_preactivation):
    sigmoid_v = jax.nn.sigmoid(gate_preactivation)
    return sigmoid_v * (1.0 + gate_preactivation * (1.0 - sigmoid_v))


def neighbours(down_slot, up_slot):
    padded = extended(jnp.stack([down_slot, up_slot]), (("section", 0),), 1)
    return (padded[3], padded[0])


def local(lat_raw, txt_raw, lat_embed, txt_embed, image_owner, text_len, weights, top_grad):
    my_shard = lax.axis_index("dp")
    section_here = lax.axis_index("section")
    section_pos = section_here % PIPE
    first_col = section_here - section_pos
    senders = jnp.argsort(image_owner, axis=1, stable=True)
    dest_order = lax.dynamic_index_in_dim(senders, section_here, 0, keepdims=False)
    text_rows = jnp.einsum(
        "jrc,cf->jrf", txt_raw[0], txt_embed, preferred_element_type=jnp.float32
    ).astype(jnp.bfloat16)
    lat_enc = jnp.einsum(
        "jrc,cf->jrf", lat_raw[0], lat_embed, preferred_element_type=jnp.float32
    ).astype(jnp.bfloat16)
    lat_payload = jnp.take(lat_enc, dest_order, axis=0)
    got_lat, got_text = (
        lax.all_to_all(lat_payload, "dp", split_axis=0, concat_axis=0, tiled=True),
        lax.all_to_all(
            jnp.take(text_rows, dest_order, axis=0), "dp", split_axis=0, concat_axis=0, tiled=True
        ),
    )
    got_lat = got_lat.reshape(-1, got_lat.shape[-1])
    feed_rows = jnp.concatenate([got_lat, got_text.reshape(-1, got_text.shape[-1])], axis=0)
    weight_part = weights[0]
    weight_fwd = lax.all_gather(weight_part, "dp", axis=0, tiled=True)
    lane_send = lax.dynamic_slice_in_dim(senders, first_col, PIPE, 0)
    lane_len = lax.dynamic_slice_in_dim(text_len, first_col, PIPE, 0)
    src_slots = lax.dynamic_index_in_dim(lane_send, my_shard, 1, keepdims=False)
    lane_lengths = jnp.take_along_axis(lane_len, src_slots[:, None], axis=1)[:, 0]
    positions = jnp.arange(feed_rows.shape[0])
    zero_rows = jnp.zeros_like(feed_rows)

    def mask_for(micro_idx):
        length = lax.dynamic_index_in_dim(
            lane_lengths, jnp.clip(micro_idx, 0, PIPE - 1), 0, keepdims=False
        )
        text_mask = ((positions >= LAT) & (positions < LAT + length)).astype(jnp.float32)
        return (text_mask, length.astype(jnp.float32))

    def forward(tokens_in, micro_idx):
        text_mask, text_count = mask_for(micro_idx)
        widened = tokens_in.astype(jnp.float32)
        hidden_layer_state = modulate(widened, text_mask, text_count).astype(jnp.bfloat16)
        gate_preactivation = jnp.dot(
            hidden_layer_state, weight_fwd, preferred_element_type=jnp.float32
        )
        return (widened + jax.nn.silu(gate_preactivation)).astype(jnp.bfloat16)

    def advance(turn_index, feed_slot, in_rows, stored):
        micro_idx = turn_index - section_pos
        active = (micro_idx >= 0) & (micro_idx < PIPE)
        tokens_in = jnp.where(section_pos == 0, feed_slot, in_rows)

        def advance_do_work(kept):
            placed = lax.dynamic_update_index_in_dim(
                kept, tokens_in, jnp.clip(micro_idx, 0, PIPE - 1), 0
            )
            return (forward(tokens_in, micro_idx), placed)

        def advance_no_work(kept):
            return (zero_rows, kept)

        return lax.cond(active, advance_do_work, advance_no_work, stored)

    final_turn = 2 * PIPE - 1
    stored = jnp.zeros((PIPE,) + feed_rows.shape, jnp.bfloat16)
    outbox, stored = advance(0, feed_rows, zero_rows, stored)

    def both_forward(turn_index, state_tuple):
        feed_slot, outbox, stored = state_tuple
        feed_slot, in_rows = neighbours(feed_slot, outbox)
        outbox, stored = advance(turn_index, feed_slot, in_rows, stored)
        return (feed_slot, outbox, stored)

    state_tuple = lax.fori_loop(1, final_turn, both_forward, (feed_rows, outbox, stored))
    stored = state_tuple[2]

    def backward(tokens_in, grad_rows, micro_idx):
        text_mask, text_count = mask_for(micro_idx)
        widened = tokens_in.astype(jnp.float32)
        hidden_wide, pullback = jax.vjp(
            lambda values: modulate(values, text_mask, text_count), widened
        )
        hidden_layer_state = hidden_wide.astype(jnp.bfloat16)
        gate_preactivation = jnp.dot(
            hidden_layer_state, weight_fwd, preferred_element_type=jnp.float32
        )
        derivative_rows = (grad_rows.astype(jnp.float32) * silu_slope(gate_preactivation)).astype(
            jnp.bfloat16
        )
        reverse_sweep = lax.dot_general(
            derivative_rows,
            weight_fwd,
            (((1,), (1,)), ((), ())),
            preferred_element_type=jnp.float32,
        )
        grad_out = (grad_rows.astype(jnp.float32) + pullback(reverse_sweep)[0]).astype(jnp.bfloat16)
        return (grad_out, hidden_layer_state, derivative_rows)

    def retreat(turn_index, grad_in, top_slot, saved_rows):
        micro_idx = turn_index - (PIPE - 1 - section_pos)
        active = (micro_idx >= 0) & (micro_idx < PIPE)
        clipped = jnp.clip(micro_idx, 0, PIPE - 1)
        grad_rows = jnp.where(section_pos == PIPE - 1, top_slot, grad_in)

        def retreat_do_work(kept):
            tokens_in = lax.dynamic_index_in_dim(stored, clipped, 0, keepdims=False)
            grad_out, hidden_layer_state, derivative_rows = backward(
                tokens_in, grad_rows, micro_idx
            )
            hiddens = lax.dynamic_update_index_in_dim(kept[0], hidden_layer_state, clipped, 0)
            slopes = lax.dynamic_update_index_in_dim(kept[1], derivative_rows, clipped, 0)
            return (grad_out, (hiddens, slopes))

        def retreat_no_work(kept):
            return (zero_rows, kept)

        return lax.cond(active, retreat_do_work, retreat_no_work, saved_rows)

    top_slot = top_grad[0, 0]
    saved_rows = (jnp.zeros_like(stored), jnp.zeros_like(stored))
    outbox, saved_rows = retreat(0, zero_rows, top_slot, saved_rows)

    def both_backward(turn_index, state_tuple):
        top_slot, outbox, saved_rows = state_tuple
        grad_in, top_slot = neighbours(outbox, top_slot)
        outbox, saved_rows = retreat(turn_index, grad_in, top_slot, saved_rows)
        return (top_slot, outbox, saved_rows)

    state_tuple = lax.fori_loop(1, final_turn, both_backward, (top_slot, outbox, saved_rows))
    hiddens, slopes = state_tuple[2]
    flat_hidden = hiddens.reshape(-1, hiddens.shape[-1])
    flat_slope = slopes.reshape(-1, slopes.shape[-1])
    my_share = lax.psum_scatter(
        lax.dot_general(
            flat_hidden, flat_slope, (((0,), (0,)), ((), ())), preferred_element_type=jnp.float32
        ).astype(jnp.bfloat16),
        "dp",
        scatter_dimension=0,
        tiled=True,
    ).astype(jnp.float32)
    return my_share[None]


def solution(mesh):
    placed = (
        P("section", None, "dp", None),
        P("section", None, "dp", None),
        P(),
        P(),
        P(),
        P(),
        P("section", "dp", None),
        P("dp", "section", None, None),
    )
    return jax.shard_map(
        local, mesh=mesh, in_specs=placed, out_specs=P("section", "dp", None), check_vma=False
    )
```

profile of v0, /device:TPU:27, one launch (start us, length us, event | category | flops | bytes accessed | tf_op | source)
XLA Modules:
  0.0 692.3 jit_solution(8392357912721677020)
XLA Ops:
  17.6 7.6 %all-to-all-start.1 = ((bf16[16,2,512]{2,1,0:T(2,128)(2,1)}), bf16[16,2,512]{2,1,0:T(2,128)(2,1)S(1)}, u32[]{:S(2)}, u32[]{:S(2)}) async-start(bf16[16,2,512]{2,1,0:T(2,128)(2,1)} %reshape.240), calls=%async_computation.1 | async-start | bytes 65536 | tf_op jit(solution)/shard_map/all_to_all | solution.py:63
  29.9 6.5 all-to-all-start
  41.1 19.9 %all-gather.3.cloned.1.call-done = bf16[1,1024,1024]{2,1,0:T(8,128)(2,1)} async-done(((bf16[1,64,1024]{2,1,0:T(8,128)(2,1)}), bf16[1,1024,1024]{2,1,0:T(8,128)(2,1)}) %all-gather.3.cloned.1.call-update) | async-done | bytes 2097168 | tf_op jit(solution)/shard_map/all_gather | solution.py:70
  62.5 198.9 %while.46 = (s32[]{:T(128)}, bf16[32,1024]{1,0:T(8,128)(2,1)S(1)}, bf16[32,1024]{1,0:T(8,128)(2,1)}, bf16[8,32,1024]{2,1,0:T(8,128)(2,1)}, s32[]{:T(128)}, /*ind...) while((s32[]{:T(128)}, bf16[32,1024]{1,0:T(8,128)(2,1)S(1)}, ...), condition=%wide.region_10.12_spmd.clone.clone, body=%wide.region_5.11_spmd.clone.clone.sunk | while | flops 67733672 | bytes 3295359 | solution.py:120
  62.5 6.4 collective-permute-start
  87.5 8.3 %collective-permute-start = (bf16[1,32,1024]{2,1,0:T(8,128)(2,1)S(1)}, bf16[1,32,1024]{2,1,0:T(8,128)(2,1)S(1)}, u32[]{:S(2)}, u32[]{:S(2)}) collective-permute-start(bf16[1,32,1024]{2,1,0:T(8,128)(2,1)S(1)} %bitcast.166), channel_id=1, source_target_pairs={{1,0},{2,1},{3,2},{4,3},{5,4},{6,5},{7,6},{8,7},{9,8},{10,9},{11,1... | collective-permute-start | bytes 196616 | tf_op jit(solution)/shard_map/while/body/eval_jaxpr/ppermute | solution.py:23
  97.7 8.2 %collective-permute-done.1 = bf16[1,32,1024]{2,1,0:T(8,128)(2,1)S(1)} collective-permute-done((bf16[1,32,1024]{2,1,0:T(8,128)(2,1)}, bf16[1,32,1024]{2,1,0:T(8,128)(2,1)S(1)}, u32[]{:S(2)}, u32[]{:S(2)}) %collective-permute-start.1) | collective-permute-done | bytes 65568 | tf_op jit(solution)/shard_map/while/body/eval_jaxpr/ppermute | solution.py:21
  106.5 8.3 %collective-permute-start = (bf16[1,32,1024]{2,1,0:T(8,128)(2,1)S(1)}, bf16[1,32,1024]{2,1,0:T(8,128)(2,1)S(1)}, u32[]{:S(2)}, u32[]{:S(2)}) collective-permute-start(bf16[1,32,1024]{2,1,0:T(8,128)(2,1)S(1)} %bitcast.166), channel_id=1, source_target_pairs={{1,0},{2,1},{3,2},{4,3},{5,4},{6,5},{7,6},{8,7},{9,8},{10,9},{11,1... | collective-permute-start | bytes 196616 | tf_op jit(solution)/shard_map/while/body/eval_jaxpr/ppermute | solution.py:23
  122.1 5.5 conditional.12
  243.0 6.2 collective-permute-start.1
  263.7 295.5 %while.47 = (s32[]{:T(128)}, bf16[32,1024]{1,0:T(8,128)(2,1)S(1)}, bf16[32,1024]{1,0:T(8,128)(2,1)}, bf16[8,32,1024]{2,1,0:T(8,128)(2,1)}, bf16[8,32,1024]{2,1,0...) while((s32[]{:T(128)}, bf16[32,1024]{1,0:T(8,128)(2,1)S(1)}, ...), condition=%wide.region_24.26_spmd.clone.clone, body=%wide.region_17.25_spmd.clone.clone.sunk | while | flops 136088896 | bytes 14930411 | solution.py:175
  263.7 6.7 collective-permute-start.2
  276.6 20.2 %collective-permute-start.2 = (bf16[1,32,1024]{2,1,0:T(8,128)(2,1)S(1)}, bf16[1,32,1024]{2,1,0:T(8,128)(2,1)S(1)}, u32[]{:S(2)}, u32[]{:S(2)}) collective-permute-start(bf16[1,32,1024]{2,1,0:T(8,128)(2,1)S(1)} %bitcast.165), channel_id=1, source_target_pairs={{0,1},{1,2},{2,3},{3,4},{4,5},{5,6},{6,7},{7,8},{8,9},{9,10},{10,1... | collective-permute-start | bytes 196616 | tf_op jit(solution)/shard_map/while/body/eval_jaxpr/ppermute | solution.py:21
  298.7 15.2 %collective-permute-done.3 = bf16[1,32,1024]{2,1,0:T(8,128)(2,1)S(1)} collective-permute-done((bf16[1,32,1024]{2,1,0:T(8,128)(2,1)}, bf16[1,32,1024]{2,1,0:T(8,128)(2,1)S(1)}, u32[]{:S(2)}, u32[]{:S(2)}) %collective-permute-start.3) | collective-permute-done | bytes 65568 | tf_op jit(solution)/shard_map/while/body/eval_jaxpr/ppermute | solution.py:23
  314.5 15.3 %collective-permute-start.2 = (bf16[1,32,1024]{2,1,0:T(8,128)(2,1)S(1)}, bf16[1,32,1024]{2,1,0:T(8,128)(2,1)S(1)}, u32[]{:S(2)}, u32[]{:S(2)}) collective-permute-start(bf16[1,32,1024]{2,1,0:T(8,128)(2,1)S(1)} %bitcast.165), channel_id=1, source_target_pairs={{0,1},{1,2},{2,3},{3,4},{4,5},{5,6},{6,7},{7,8},{8,9},{9,10},{10,1... | collective-permute-start | bytes 196616 | tf_op jit(solution)/shard_map/while/body/eval_jaxpr/ppermute | solution.py:21
  335.1 12.6 %conditional.13 = (bf16[32,1024]{1,0:T(8,128)(2,1)}, bf16[8,32,1024]{2,1,0:T(8,128)(2,1)}, bf16[8,32,1024]{2,1,0:T(8,128)(2,1)}) conditional(s32[]{:T(128)} %convert_element_type.366, (bf16[8,32,1024]{2,1,0:T(8,128)(2,1)}, bf16[8,32,1024]{2,1,0:T(8,128)(2,1)}) %tuple.144, (pred[]{:T(512)}, bf16[1,32,1024]{2,1,0:T(8,128)(2,1)S(1)}, ...), branch_computations={%region_18.19_spmd, %region_19.24_spmd} | conditional | flops 136088896 | bytes 14274576 | solution.py:163
  356.7 12.6 %conditional.13 = (bf16[32,1024]{1,0:T(8,128)(2,1)}, bf16[8,32,1024]{2,1,0:T(8,128)(2,1)}, bf16[8,32,1024]{2,1,0:T(8,128)(2,1)}) conditional(s32[]{:T(128)} %convert_element_type.366, (bf16[8,32,1024]{2,1,0:T(8,128)(2,1)}, bf16[8,32,1024]{2,1,0:T(8,128)(2,1)}) %tuple.144, (pred[]{:T(512)}, bf16[1,32,1024]{2,1,0:T(8,128)(2,1)S(1)}, ...), branch_computations={%region_18.19_spmd, %region_19.24_spmd} | conditional | flops 136088896 | bytes 14274576 | solution.py:163
  378.5 12.6 %conditional.13 = (bf16[32,1024]{1,0:T(8,128)(2,1)}, bf16[8,32,1024]{2,1,0:T(8,128)(2,1)}, bf16[8,32,1024]{2,1,0:T(8,128)(2,1)}) conditional(s32[]{:T(128)} %convert_element_type.366, (bf16[8,32,1024]{2,1,0:T(8,128)(2,1)}, bf16[8,32,1024]{2,1,0:T(8,128)(2,1)}) %tuple.144, (pred[]{:T(512)}, bf16[1,32,1024]{2,1,0:T(8,128)(2,1)S(1)}, ...), branch_computations={%region_18.19_spmd, %region_19.24_spmd} | conditional | flops 136088896 | bytes 14274576 | solution.py:163
  400.3 12.6 %conditional.13 = (bf16[32,1024]{1,0:T(8,128)(2,1)}, bf16[8,32,1024]{2,1,0:T(8,128)(2,1)}, bf16[8,32,1024]{2,1,0:T(8,128)(2,1)}) conditional(s32[]{:T(128)} %convert_element_type.366, (bf16[8,32,1024]{2,1,0:T(8,128)(2,1)}, bf16[8,32,1024]{2,1,0:T(8,128)(2,1)}) %tuple.144, (pred[]{:T(512)}, bf16[1,32,1024]{2,1,0:T(8,128)(2,1)S(1)}, ...), branch_computations={%region_18.19_spmd, %region_19.24_spmd} | conditional | flops 136088896 | bytes 14274576 | solution.py:163
  414.8 5.7 collective-permute-start.3
  422.1 12.6 %conditional.13 = (bf16[32,1024]{1,0:T(8,128)(2,1)}, bf16[8,32,1024]{2,1,0:T(8,128)(2,1)}, bf16[8,32,1024]{2,1,0:T(8,128)(2,1)}) conditional(s32[]{:T(128)} %convert_element_type.366, (bf16[8,32,1024]{2,1,0:T(8,128)(2,1)}, bf16[8,32,1024]{2,1,0:T(8,128)(2,1)}) %tuple.144, (pred[]{:T(512)}, bf16[1,32,1024]{2,1,0:T(8,128)(2,1)S(1)}, ...), branch_computations={%region_18.19_spmd, %region_19.24_spmd} | conditional | flops 136088896 | bytes 14274576 | solution.py:163
  436.6 5.7 collective-permute-start.3
  444.0 12.6 %conditional.13 = (bf16[32,1024]{1,0:T(8,128)(2,1)}, bf16[8,32,1024]{2,1,0:T(8,128)(2,1)}, bf16[8,32,1024]{2,1,0:T(8,128)(2,1)}) conditional(s32[]{:T(128)} %convert_element_type.366, (bf16[8,32,1024]{2,1,0:T(8,128)(2,1)}, bf16[8,32,1024]{2,1,0:T(8,128)(2,1)}) %tuple.144, (pred[]{:T(512)}, bf16[1,32,1024]{2,1,0:T(8,128)(2,1)S(1)}, ...), branch_computations={%region_18.19_spmd, %region_19.24_spmd} | conditional | flops 136088896 | bytes 14274576 | solution.py:163
  458.5 5.7 collective-permute-start.3
  465.8 12.6 %conditional.13 = (bf16[32,1024]{1,0:T(8,128)(2,1)}, bf16[8,32,1024]{2,1,0:T(8,128)(2,1)}, bf16[8,32,1024]{2,1,0:T(8,128)(2,1)}) conditional(s32[]{:T(128)} %convert_element_type.366, (bf16[8,32,1024]{2,1,0:T(8,128)(2,1)}, bf16[8,32,1024]{2,1,0:T(8,128)(2,1)}) %tuple.144, (pred[]{:T(512)}, bf16[1,32,1024]{2,1,0:T(8,128)(2,1)S(1)}, ...), branch_computations={%region_18.19_spmd, %region_19.24_spmd} | conditional | flops 136088896 | bytes 14274576 | solution.py:163
  480.3 5.7 collective-permute-start.3
  487.6 12.6 %conditional.13 = (bf16[32,1024]{1,0:T(8,128)(2,1)}, bf16[8,32,1024]{2,1,0:T(8,128)(2,1)}, bf16[8,32,1024]{2,1,0:T(8,128)(2,1)}) conditional(s32[]{:T(128)} %convert_element_type.366, (bf16[8,32,1024]{2,1,0:T(8,128)(2,1)}, bf16[8,32,1024]{2,1,0:T(8,128)(2,1)}) %tuple.144, (pred[]{:T(512)}, bf16[1,32,1024]{2,1,0:T(8,128)(2,1)S(1)}, ...), branch_computations={%region_18.19_spmd, %region_19.24_spmd} | conditional | flops 136088896 | bytes 14274576 | solution.py:163
  502.1 5.7 collective-permute-start.3
  512.0 17.6 %collective-permute-start.3 = (bf16[1,32,1024]{2,1,0:T(8,128)(2,1)}, bf16[1,32,1024]{2,1,0:T(8,128)(2,1)S(1)}, u32[]{:S(2)}, u32[]{:S(2)}) collective-permute-start(bf16[1,32,1024]{2,1,0:T(8,128)(2,1)} %bitcast.156), channel_id=1, source_target_pairs={{1,0},{2,1},{3,2},{4,3},{5,4},{6,5},{7,6},{8,7},{9,8},{10,9},{11,1... | collective-permute-start | bytes 196616 | tf_op jit(solution)/shard_map/while/body/eval_jaxpr/ppermute | solution.py:23
  533.8 5.7 collective-permute-start.3
  543.7 13.2 %collective-permute-start.3 = (bf16[1,32,1024]{2,1,0:T(8,128)(2,1)}, bf16[1,32,1024]{2,1,0:T(8,128)(2,1)S(1)}, u32[]{:S(2)}, u32[]{:S(2)}) collective-permute-start(bf16[1,32,1024]{2,1,0:T(8,128)(2,1)} %bitcast.156), channel_id=1, source_target_pairs={{1,0},{2,1},{3,2},{4,3},{5,4},{6,5},{7,6},{8,7},{9,8},{10,9},{11,1... | collective-permute-start | bytes 196616 | tf_op jit(solution)/shard_map/while/body/eval_jaxpr/ppermute | solution.py:23
  562.5 121.4 %reduce-scatter.2.cloned.1.call-done = bf16[64,1024]{1,0:T(8,128)(2,1)} async-done(((bf16[1024,1024]{1,0:T(8,128)(2,1)}), bf16[64,1024]{1,0:T(8,128)(2,1)}) %reduce-scatter.2.cloned.1.call-update) | async-done | bytes 131088 | tf_op jit(solution)/shard_map/reduce_scatter | solution.py:179
  (417 shorter events, 391.5 us)
Async XLA Ops:
  6.5 54.4 %all-gather.3.cloned.1.call-start = ((), (), s32[]{:S(2)}) async-start(), calls=%async_computation.4 | async-start | bytes 2228224 | tf_op jit(solution)/shard_map/all_gather | solution.py:70
  17.6 12.2 %all-to-all-start.1 = ((bf16[16,2,512]{2,1,0:T(2,128)(2,1)}), bf16[16,2,512]{2,1,0:T(2,128)(2,1)S(1)}, u32[]{:S(2)}, u32[]{:S(2)}) async-start(bf16[16,2,512]{2,1,0:T(2,128)(2,1)} %reshape.240), calls=%async_computation.1 | async-start | bytes 65536 | tf_op jit(solution)/shard_map/all_to_all | solution.py:63
  29.9 11.1 %all-to-all-start = ((bf16[16,2,512]{2,1,0:T(2,128)(2,1)}), bf16[16,2,512]{2,1,0:T(2,128)(2,1)S(1)}, u32[]{:S(2)}, u32[]{:S(2)}) async-start(bf16[16,2,512]{2,1,0:T(2,128)(2,1)} %reshape.242), calls=%async_computation | async-start | bytes 65536 | tf_op jit(solution)/shard_map/all_to_all | solution.py:62
  36.4 647.5 %reduce-scatter.2.cloned.1.call-start = ((), (), s32[]{:S(2)}) async-start(), calls=%async_computation.3 | async-start | bytes 2228224 | tf_op jit(solution)/shard_map/reduce_scatter | solution.py:179
  62.5 8.4 %collective-permute-start = (bf16[1,32,1024]{2,1,0:T(8,128)(2,1)S(1)}, bf16[1,32,1024]{2,1,0:T(8,128)(2,1)S(1)}, u32[]{:S(2)}, u32[]{:S(2)}) collective-permute-start(bf16[1,32,1024]{2,1,0:T(8,128)(2,1)S(1)} %bitcast.166), channel_id=1, source_target_pairs={{1,0},{2,1},{3,2},{4,3},{5,4},{6,5},{7,6},{8,7},{9,8},{10,9},{11,1... | collective-permute-start | bytes 196616 | tf_op jit(solution)/shard_map/while/body/eval_jaxpr/ppermute | solution.py:23
  78.8 8.1 %collective-permute-start.1 = (bf16[1,32,1024]{2,1,0:T(8,128)(2,1)}, bf16[1,32,1024]{2,1,0:T(8,128)(2,1)S(1)}, u32[]{:S(2)}, u32[]{:S(2)}) collective-permute-start(bf16[1,32,1024]{2,1,0:T(8,128)(2,1)} %bitcast.153), channel_id=1, source_target_pairs={{0,1},{1,2},{2,3},{3,4},{4,5},{5,6},{6,7},{7,8},{8,9},{9,10},{10,1... | collective-permute-start | bytes 196616 | tf_op jit(solution)/shard_map/while/body/eval_jaxpr/ppermute | solution.py:21
  87.5 10.2 %collective-permute-start = (bf16[1,32,1024]{2,1,0:T(8,128)(2,1)S(1)}, bf16[1,32,1024]{2,1,0:T(8,128)(2,1)S(1)}, u32[]{:S(2)}, u32[]{:S(2)}) collective-permute-start(bf16[1,32,1024]{2,1,0:T(8,128)(2,1)S(1)} %bitcast.166), channel_id=1, source_target_pairs={{1,0},{2,1},{3,2},{4,3},{5,4},{6,5},{7,6},{8,7},{9,8},{10,9},{11,1... | collective-permute-start | bytes 196616 | tf_op jit(solution)/shard_map/while/body/eval_jaxpr/ppermute | solution.py:23
  95.8 10.1 %collective-permute-start.1 = (bf16[1,32,1024]{2,1,0:T(8,128)(2,1)}, bf16[1,32,1024]{2,1,0:T(8,128)(2,1)S(1)}, u32[]{:S(2)}, u32[]{:S(2)}) collective-permute-start(bf16[1,32,1024]{2,1,0:T(8,128)(2,1)} %bitcast.153), channel_id=1, source_target_pairs={{0,1},{1,2},{2,3},{3,4},{4,5},{5,6},{6,7},{7,8},{8,9},{9,10},{10,1... | collective-permute-start | bytes 196616 | tf_op jit(solution)/shard_map/while/body/eval_jaxpr/ppermute | solution.py:21
  106.5 10.2 %collective-permute-start = (bf16[1,32,1024]{2,1,0:T(8,128)(2,1)S(1)}, bf16[1,32,1024]{2,1,0:T(8,128)(2,1)S(1)}, u32[]{:S(2)}, u32[]{:S(2)}) collective-permute-start(bf16[1,32,1024]{2,1,0:T(8,128)(2,1)S(1)} %bitcast.166), channel_id=1, source_target_pairs={{1,0},{2,1},{3,2},{4,3},{5,4},{6,5},{7,6},{8,7},{9,8},{10,9},{11,1... | collective-permute-start | bytes 196616 | tf_op jit(solution)/shard_map/while/body/eval_jaxpr/ppermute | solution.py:23
  114.8 7.3 %collective-permute-start.1 = (bf16[1,32,1024]{2,1,0:T(8,128)(2,1)}, bf16[1,32,1024]{2,1,0:T(8,128)(2,1)S(1)}, u32[]{:S(2)}, u32[]{:S(2)}) collective-permute-start(bf16[1,32,1024]{2,1,0:T(8,128)(2,1)} %bitcast.153), channel_id=1, source_target_pairs={{0,1},{1,2},{2,3},{3,4},{4,5},{5,6},{6,7},{7,8},{8,9},{9,10},{10,1... | collective-permute-start | bytes 196616 | tf_op jit(solution)/shard_map/while/body/eval_jaxpr/ppermute | solution.py:21
  241.1 8.1 %collective-permute-start = (bf16[1,32,1024]{2,1,0:T(8,128)(2,1)S(1)}, bf16[1,32,1024]{2,1,0:T(8,128)(2,1)S(1)}, u32[]{:S(2)}, u32[]{:S(2)}) collective-permute-start(bf16[1,32,1024]{2,1,0:T(8,128)(2,1)S(1)} %bitcast.166), channel_id=1, source_target_pairs={{1,0},{2,1},{3,2},{4,3},{5,4},{6,5},{7,6},{8,7},{9,8},{10,9},{11,1... | collective-permute-start | bytes 196616 | tf_op jit(solution)/shard_map/while/body/eval_jaxpr/ppermute | solution.py:23
  243.0 7.8 %collective-permute-start.1 = (bf16[1,32,1024]{2,1,0:T(8,128)(2,1)}, bf16[1,32,1024]{2,1,0:T(8,128)(2,1)S(1)}, u32[]{:S(2)}, u32[]{:S(2)}) collective-permute-start(bf16[1,32,1024]{2,1,0:T(8,128)(2,1)} %bitcast.153), channel_id=1, source_target_pairs={{0,1},{1,2},{2,3},{3,4},{4,5},{5,6},{6,7},{7,8},{8,9},{9,10},{10,1... | collective-permute-start | bytes 196616 | tf_op jit(solution)/shard_map/while/body/eval_jaxpr/ppermute | solution.py:21
  263.7 8.7 %collective-permute-start.2 = (bf16[1,32,1024]{2,1,0:T(8,128)(2,1)S(1)}, bf16[1,32,1024]{2,1,0:T(8,128)(2,1)S(1)}, u32[]{:S(2)}, u32[]{:S(2)}) collective-permute-start(bf16[1,32,1024]{2,1,0:T(8,128)(2,1)S(1)} %bitcast.165), channel_id=1, source_target_pairs={{0,1},{1,2},{2,3},{3,4},{4,5},{5,6},{6,7},{7,8},{8,9},{9,10},{10,1... | collective-permute-start | bytes 196616 | tf_op jit(solution)/shard_map/while/body/eval_jaxpr/ppermute | solution.py:21
  276.6 22.1 %collective-permute-start.2 = (bf16[1,32,1024]{2,1,0:T(8,128)(2,1)S(1)}, bf16[1,32,1024]{2,1,0:T(8,128)(2,1)S(1)}, u32[]{:S(2)}, u32[]{:S(2)}) collective-permute-start(bf16[1,32,1024]{2,1,0:T(8,128)(2,1)S(1)} %bitcast.165), channel_id=1, source_target_pairs={{0,1},{1,2},{2,3},{3,4},{4,5},{5,6},{6,7},{7,8},{8,9},{9,10},{10,1... | collective-permute-start | bytes 196616 | tf_op jit(solution)/shard_map/while/body/eval_jaxpr/ppermute | solution.py:21
  296.7 17.2 %collective-permute-start.3 = (bf16[1,32,1024]{2,1,0:T(8,128)(2,1)}, bf16[1,32,1024]{2,1,0:T(8,128)(2,1)S(1)}, u32[]{:S(2)}, u32[]{:S(2)}) collective-permute-start(bf16[1,32,1024]{2,1,0:T(8,128)(2,1)} %bitcast.156), channel_id=1, source_target_pairs={{1,0},{2,1},{3,2},{4,3},{5,4},{6,5},{7,6},{8,7},{9,8},{10,9},{11,1... | collective-permute-start | bytes 196616 | tf_op jit(solution)/shard_map/while/body/eval_jaxpr/ppermute | solution.py:23
  314.5 17.2 %collective-permute-start.2 = (bf16[1,32,1024]{2,1,0:T(8,128)(2,1)S(1)}, bf16[1,32,1024]{2,1,0:T(8,128)(2,1)S(1)}, u32[]{:S(2)}, u32[]{:S(2)}) collective-permute-start(bf16[1,32,1024]{2,1,0:T(8,128)(2,1)S(1)} %bitcast.165), channel_id=1, source_target_pairs={{0,1},{1,2},{2,3},{3,4},{4,5},{5,6},{6,7},{7,8},{8,9},{9,10},{10,1... | collective-permute-start | bytes 196616 | tf_op jit(solution)/shard_map/while/body/eval_jaxpr/ppermute | solution.py:21
  347.6 7.4 %collective-permute-start.2 = (bf16[1,32,1024]{2,1,0:T(8,128)(2,1)S(1)}, bf16[1,32,1024]{2,1,0:T(8,128)(2,1)S(1)}, u32[]{:S(2)}, u32[]{:S(2)}) collective-permute-start(bf16[1,32,1024]{2,1,0:T(8,128)(2,1)S(1)} %bitcast.165), channel_id=1, source_target_pairs={{0,1},{1,2},{2,3},{3,4},{4,5},{5,6},{6,7},{7,8},{8,9},{9,10},{10,1... | collective-permute-start | bytes 196616 | tf_op jit(solution)/shard_map/while/body/eval_jaxpr/ppermute | solution.py:21
  369.2 7.6 %collective-permute-start.2 = (bf16[1,32,1024]{2,1,0:T(8,128)(2,1)S(1)}, bf16[1,32,1024]{2,1,0:T(8,128)(2,1)S(1)}, u32[]{:S(2)}, u32[]{:S(2)}) collective-permute-start(bf16[1,32,1024]{2,1,0:T(8,128)(2,1)S(1)} %bitcast.165), channel_id=1, source_target_pairs={{0,1},{1,2},{2,3},{3,4},{4,5},{5,6},{6,7},{7,8},{8,9},{9,10},{10,1... | collective-permute-start | bytes 196616 | tf_op jit(solution)/shard_map/while/body/eval_jaxpr/ppermute | solution.py:21
  391.0 7.6 %collective-permute-start.2 = (bf16[1,32,1024]{2,1,0:T(8,128)(2,1)S(1)}, bf16[1,32,1024]{2,1,0:T(8,128)(2,1)S(1)}, u32[]{:S(2)}, u32[]{:S(2)}) collective-permute-start(bf16[1,32,1024]{2,1,0:T(8,128)(2,1)S(1)} %bitcast.165), channel_id=1, source_target_pairs={{0,1},{1,2},{2,3},{3,4},{4,5},{5,6},{6,7},{7,8},{8,9},{9,10},{10,1... | collective-permute-start | bytes 196616 | tf_op jit(solution)/shard_map/while/body/eval_jaxpr/ppermute | solution.py:21
  412.9 7.6 %collective-permute-start.2 = (bf16[1,32,1024]{2,1,0:T(8,128)(2,1)S(1)}, bf16[1,32,1024]{2,1,0:T(8,128)(2,1)S(1)}, u32[]{:S(2)}, u32[]{:S(2)}) collective-permute-start(bf16[1,32,1024]{2,1,0:T(8,128)(2,1)S(1)} %bitcast.165), channel_id=1, source_target_pairs={{0,1},{1,2},{2,3},{3,4},{4,5},{5,6},{6,7},{7,8},{8,9},{9,10},{10,1... | collective-permute-start | bytes 196616 | tf_op jit(solution)/shard_map/while/body/eval_jaxpr/ppermute | solution.py:21
  434.7 7.7 %collective-permute-start.2 = (bf16[1,32,1024]{2,1,0:T(8,128)(2,1)S(1)}, bf16[1,32,1024]{2,1,0:T(8,128)(2,1)S(1)}, u32[]{:S(2)}, u32[]{:S(2)}) collective-permute-start(bf16[1,32,1024]{2,1,0:T(8,128)(2,1)S(1)} %bitcast.165), channel_id=1, source_target_pairs={{0,1},{1,2},{2,3},{3,4},{4,5},{5,6},{6,7},{7,8},{8,9},{9,10},{10,1... | collective-permute-start | bytes 196616 | tf_op jit(solution)/shard_map/while/body/eval_jaxpr/ppermute | solution.py:21
  436.6 7.4 %collective-permute-start.3 = (bf16[1,32,1024]{2,1,0:T(8,128)(2,1)}, bf16[1,32,1024]{2,1,0:T(8,128)(2,1)S(1)}, u32[]{:S(2)}, u32[]{:S(2)}) collective-permute-start(bf16[1,32,1024]{2,1,0:T(8,128)(2,1)} %bitcast.156), channel_id=1, source_target_pairs={{1,0},{2,1},{3,2},{4,3},{5,4},{6,5},{7,6},{8,7},{9,8},{10,9},{11,1... | collective-permute-start | bytes 196616 | tf_op jit(solution)/shard_map/while/body/eval_jaxpr/ppermute | solution.py:23
  456.5 7.6 %collective-permute-start.2 = (bf16[1,32,1024]{2,1,0:T(8,128)(2,1)S(1)}, bf16[1,32,1024]{2,1,0:T(8,128)(2,1)S(1)}, u32[]{:S(2)}, u32[]{:S(2)}) collective-permute-start(bf16[1,32,1024]{2,1,0:T(8,128)(2,1)S(1)} %bitcast.165), channel_id=1, source_target_pairs={{0,1},{1,2},{2,3},{3,4},{4,5},{5,6},{6,7},{7,8},{8,9},{9,10},{10,1... | collective-permute-start | bytes 196616 | tf_op jit(solution)/shard_map/while/body/eval_jaxpr/ppermute | solution.py:21
  478.4 7.6 %collective-permute-start.2 = (bf16[1,32,1024]{2,1,0:T(8,128)(2,1)S(1)}, bf16[1,32,1024]{2,1,0:T(8,128)(2,1)S(1)}, u32[]{:S(2)}, u32[]{:S(2)}) collective-permute-start(bf16[1,32,1024]{2,1,0:T(8,128)(2,1)S(1)} %bitcast.165), channel_id=1, source_target_pairs={{0,1},{1,2},{2,3},{3,4},{4,5},{5,6},{6,7},{7,8},{8,9},{9,10},{10,1... | collective-permute-start | bytes 196616 | tf_op jit(solution)/shard_map/while/body/eval_jaxpr/ppermute | solution.py:21
  500.2 7.6 %collective-permute-start.2 = (bf16[1,32,1024]{2,1,0:T(8,128)(2,1)S(1)}, bf16[1,32,1024]{2,1,0:T(8,128)(2,1)S(1)}, u32[]{:S(2)}, u32[]{:S(2)}) collective-permute-start(bf16[1,32,1024]{2,1,0:T(8,128)(2,1)S(1)} %bitcast.165), channel_id=1, source_target_pairs={{0,1},{1,2},{2,3},{3,4},{4,5},{5,6},{6,7},{7,8},{8,9},{9,10},{10,1... | collective-permute-start | bytes 196616 | tf_op jit(solution)/shard_map/while/body/eval_jaxpr/ppermute | solution.py:21
  502.1 7.3 %collective-permute-start.3 = (bf16[1,32,1024]{2,1,0:T(8,128)(2,1)}, bf16[1,32,1024]{2,1,0:T(8,128)(2,1)S(1)}, u32[]{:S(2)}, u32[]{:S(2)}) collective-permute-start(bf16[1,32,1024]{2,1,0:T(8,128)(2,1)} %bitcast.156), channel_id=1, source_target_pairs={{1,0},{2,1},{3,2},{4,3},{5,4},{6,5},{7,6},{8,7},{9,8},{10,9},{11,1... | collective-permute-start | bytes 196616 | tf_op jit(solution)/shard_map/while/body/eval_jaxpr/ppermute | solution.py:23
  510.1 19.6 %collective-permute-start.2 = (bf16[1,32,1024]{2,1,0:T(8,128)(2,1)S(1)}, bf16[1,32,1024]{2,1,0:T(8,128)(2,1)S(1)}, u32[]{:S(2)}, u32[]{:S(2)}) collective-permute-start(bf16[1,32,1024]{2,1,0:T(8,128)(2,1)S(1)} %bitcast.165), channel_id=1, source_target_pairs={{0,1},{1,2},{2,3},{3,4},{4,5},{5,6},{6,7},{7,8},{8,9},{9,10},{10,1... | collective-permute-start | bytes 196616 | tf_op jit(solution)/shard_map/while/body/eval_jaxpr/ppermute | solution.py:21
  512.0 19.3 %collective-permute-start.3 = (bf16[1,32,1024]{2,1,0:T(8,128)(2,1)}, bf16[1,32,1024]{2,1,0:T(8,128)(2,1)S(1)}, u32[]{:S(2)}, u32[]{:S(2)}) collective-permute-start(bf16[1,32,1024]{2,1,0:T(8,128)(2,1)} %bitcast.156), channel_id=1, source_target_pairs={{1,0},{2,1},{3,2},{4,3},{5,4},{6,5},{7,6},{8,7},{9,8},{10,9},{11,1... | collective-permute-start | bytes 196616 | tf_op jit(solution)/shard_map/while/body/eval_jaxpr/ppermute | solution.py:23
  531.9 7.6 %collective-permute-start.2 = (bf16[1,32,1024]{2,1,0:T(8,128)(2,1)S(1)}, bf16[1,32,1024]{2,1,0:T(8,128)(2,1)S(1)}, u32[]{:S(2)}, u32[]{:S(2)}) collective-permute-start(bf16[1,32,1024]{2,1,0:T(8,128)(2,1)S(1)} %bitcast.165), channel_id=1, source_target_pairs={{0,1},{1,2},{2,3},{3,4},{4,5},{5,6},{6,7},{7,8},{8,9},{9,10},{10,1... | collective-permute-start | bytes 196616 | tf_op jit(solution)/shard_map/while/body/eval_jaxpr/ppermute | solution.py:21
  533.8 7.3 %collective-permute-start.3 = (bf16[1,32,1024]{2,1,0:T(8,128)(2,1)}, bf16[1,32,1024]{2,1,0:T(8,128)(2,1)S(1)}, u32[]{:S(2)}, u32[]{:S(2)}) collective-permute-start(bf16[1,32,1024]{2,1,0:T(8,128)(2,1)} %bitcast.156), channel_id=1, source_target_pairs={{1,0},{2,1},{3,2},{4,3},{5,4},{6,5},{7,6},{8,7},{9,8},{10,9},{11,1... | collective-permute-start | bytes 196616 | tf_op jit(solution)/shard_map/while/body/eval_jaxpr/ppermute | solution.py:23
  541.8 15.1 %collective-permute-start.2 = (bf16[1,32,1024]{2,1,0:T(8,128)(2,1)S(1)}, bf16[1,32,1024]{2,1,0:T(8,128)(2,1)S(1)}, u32[]{:S(2)}, u32[]{:S(2)}) collective-permute-start(bf16[1,32,1024]{2,1,0:T(8,128)(2,1)S(1)} %bitcast.165), channel_id=1, source_target_pairs={{0,1},{1,2},{2,3},{3,4},{4,5},{5,6},{6,7},{7,8},{8,9},{9,10},{10,1... | collective-permute-start | bytes 196616 | tf_op jit(solution)/shard_map/while/body/eval_jaxpr/ppermute | solution.py:21
  543.7 14.8 %collective-permute-start.3 = (bf16[1,32,1024]{2,1,0:T(8,128)(2,1)}, bf16[1,32,1024]{2,1,0:T(8,128)(2,1)S(1)}, u32[]{:S(2)}, u32[]{:S(2)}) collective-permute-start(bf16[1,32,1024]{2,1,0:T(8,128)(2,1)} %bitcast.156), channel_id=1, source_target_pairs={{1,0},{2,1},{3,2},{4,3},{5,4},{6,5},{7,6},{8,7},{9,8},{10,9},{11,1... | collective-permute-start | bytes 196616 | tf_op jit(solution)/shard_map/while/body/eval_jaxpr/ppermute | solution.py:23
  (38 other events, 252.3 us)
Sparse Core Ops, SparseCore 0:
  9.7 51.1 all-gather.2
  562.6 121.1 reduce-scatter.1
where the time goes:
time: 697 us; the launch traced here: 692 us
  starting transfers between devices  255 us (37%)
  waiting for transfers between devices  248 us (36%)
  matrix products  65.9 us (9%)
  other arithmetic  61.6 us (9%)
  local copies, waits for them, and re-layouts  26.1 us (4%)
  loops' own time  22.6 us (3%)
  between operations  13.5 us (2%)
    ppermute x28, starting transfers between devices, extended(): lax.ppermute(head, axis, [((i + 1) % count, i) for i in range(ends)])  129 us
    reduce_scatter x1, waiting for transfers between devices, local(): lax.psum_scatter(lax.dot_general(flat_hidden, flat_slope, (((0,), (0,)),...  121 us
    ppermute x28, starting transfers between devices, extended(): lax.ppermute(tail, axis, [(i, (i + 1) % count) for i in range(ends)])  112 us
    ppermute x28, waiting for transfers between devices, extended(): lax.ppermute(tail, axis, [(i, (i + 1) % count) for i in range(ends)])  60.3 us
    ppermute x28, waiting for transfers between devices, extended(): lax.ppermute(head, axis, [((i + 1) % count, i) for i in range(ends)])  39.4 us
    dot_general x8, matrix products, backward(): jnp.dot(hidden_layer_state, weight_fwd, preferred_element_type=jnp.float32)  22.4 us
    dot_general x8, matrix products, forward(): jnp.dot(hidden_layer_state, weight_fwd, preferred_element_type=jnp.float32)  22.1 us
    all_gather x1, waiting for transfers between devices, local(): weight_fwd = lax.all_gather(weight_part, 'dp', axis=0, tiled=True)  19.9 us
  transfers between devices with their start and end apart: 60, of which 32 were waited for; matrix products, arithmetic and copies ran while one was open for 2% of the time, Pallas kernels for 0%

commit v1 on v0

v1 whole, which is shorter than its diff:
```python
import functools

import jax
import jax.numpy as jnp
from jax import lax
from jax.experimental import pallas as pl
from jax.experimental.pallas import tpu as pltpu
from jax.sharding import PartitionSpec as P

PIPE = 8
EPS = 1e-06
MESH = pl.DeviceIdType.MESH
F32 = jnp.float32
BF16 = jnp.bfloat16
CHUNKS = 8
HALVES = 2


def dot(a, b, ca=1, cb=0):
    return lax.dot_general(a, b, (((ca,), (cb,)), ((), ())), preferred_element_type=F32)


def kernel(
    n_dp,
    lat_ref,
    txt_ref,
    late_ref,
    txte_ref,
    own_ref,
    len_ref,
    w_ref,
    top_ref,
    out_ref,
    txte,
    wfull,
    stage_src,
    stage_dst,
    image,
    maskw,
    x_in,
    x_out,
    g_in,
    g_out,
    hid,
    slp,
    slope_s,
    u_s,
    r_s,
    q_s,
    dw,
    pair_src,
    pair_dst,
    ring_src,
    ring_dst,
    txte_sem,
    own_sem,
    agr_send,
    agr_recv,
    agl_send,
    agl_recv,
    agp_send,
    agp_recv,
    a2a_send,
    a2a_recv,
    x_send,
    x_recv,
    g_send,
    g_recv,
    feed_send,
    top_send,
    pr_send,
    pr_recv,
    rr_send,
    rr_recv,
    rl_send,
    rl_recv,
):
    ny = n_dp // 2
    n_right = ny // 2
    n_left = ny - 1 - n_right
    dp = lax.axis_index("dp")
    sec = lax.axis_index("section")
    pos = lax.rem(sec, PIPE)
    first = sec - pos
    y = lax.div(dp, 2)
    c = lax.rem(dp, 2)
    partner = 2 * y + (1 - c)
    up = 2 * lax.rem(y + 1, ny) + c
    down = 2 * lax.rem(y + ny - 1, ny) + c
    rows = w_ref.shape[0]
    width = w_ref.shape[1]
    sub = rows // HALVES
    chunk = txte_ref.shape[0] // CHUNKS

    barrier = pltpu.get_barrier_semaphore()

    def greet_dp(k, carry):
        pl.semaphore_signal(
            barrier,
            inc=1,
            device_id={"dp": lax.rem(dp + k, n_dp), "section": sec},
            device_id_type=MESH,
        )
        return carry

    def greet_sec(k, carry):
        pl.semaphore_signal(
            barrier,
            inc=1,
            device_id={"dp": dp, "section": first + lax.rem(pos + k, PIPE)},
            device_id_type=MESH,
        )
        return carry

    lax.fori_loop(1, n_dp, greet_dp, 0)
    lax.fori_loop(1, PIPE, greet_sec, 0)

    def embed_copy(i):
        return pltpu.make_async_copy(
            txte_ref.at[pl.ds(i * chunk, chunk)], txte.at[pl.ds(i * chunk, chunk)], txte_sem.at[i]
        )

    for i in range(CHUNKS):
        embed_copy(i).start()

    def at_dp(d):
        return {"dp": d, "section": sec}

    def at_pos(k):
        return {"dp": dp, "section": first + k}

    def w_rows(block, h):
        return wfull.at[pl.ds(pl.multiple_of(block * rows + h * sub, sub), sub)]

    own_copy = pltpu.make_async_copy(
        w_ref, wfull.at[pl.ds(pl.multiple_of(dp * rows, rows), rows)], own_sem
    )
    own_copy.start()

    owners = own_ref[...]
    lane = lax.broadcasted_iota(jnp.int32, owners.shape, 1)
    owner_col = jnp.sum(jnp.where(lane == sec, owners, 0), axis=1, keepdims=True)
    pick = (
        owner_col == lax.broadcasted_iota(jnp.int32, (n_dp, n_dp), 1)
    ).astype(F32)
    counts = jnp.sum(jnp.where(owners == dp, len_ref[...], 0), axis=0, keepdims=True)
    lane_row = lax.broadcasted_iota(jnp.int32, counts.shape, 1)
    half_rows = image.shape[0] // 2
    place = lax.broadcasted_iota(jnp.int32, (image.shape[0], 128), 0) - half_rows

    def mask_step(m, carry):
        count = jnp.sum(jnp.where(lane_row == first + m, counts, 0), axis=1, keepdims=True)
        inside = (place >= 0) & (place < count)
        maskw[m] = jnp.where(inside, 0.5 / count.astype(F32), 0.0)
        return carry

    lax.fori_loop(0, PIPE, mask_step, 0)

    lat_enc = dot(lat_ref[...], late_ref[...]).astype(BF16)

    acc = jnp.zeros((n_dp, width), F32)
    for i in range(CHUNKS):
        embed_copy(i).wait()
        acc += dot(txt_ref[:, i * chunk : (i + 1) * chunk], txte[i * chunk : (i + 1) * chunk, :])
    pick = pick.astype(BF16)
    stage_src[:, 0, 0:width] = dot(pick, lat_enc, 0, 0)
    stage_src[:, 0, width : 2 * width] = dot(pick, acc.astype(BF16), 0, 0)

    pl.semaphore_wait(barrier, n_dp - 1 + PIPE - 1)

    def right_copy(t, h):
        block = 2 * lax.rem(y + ny - t, ny) + c
        src = w_ref.at[pl.ds(h * sub, sub)] if t == 0 else w_rows(block, h)
        return pltpu.make_async_remote_copy(
            src, w_rows(block, h), agr_send.at[t, h], agr_recv.at[t, h], at_dp(up), MESH
        )

    def left_copy(t, h):
        block = 2 * lax.rem(y + t, ny) + c
        src = w_ref.at[pl.ds(h * sub, sub)] if t == 0 else w_rows(block, h)
        return pltpu.make_async_remote_copy(
            src, w_rows(block, h), agl_send.at[t, h], agl_recv.at[t, h], at_dp(down), MESH
        )

    def pair_copy(i, block_y, h):
        block = 2 * block_y + c
        src = w_ref.at[pl.ds(h * sub, sub)] if i == 0 else w_rows(block, h)
        return pltpu.make_async_remote_copy(
            src, w_rows(block, h), agp_send.at[i, h], agp_recv.at[i, h], at_dp(partner), MESH
        )

    def from_right_going(t):
        return lax.rem(y + ny - t, ny)

    def from_left_going(t):
        return lax.rem(y + t, ny)

    def gather_step(t):
        for h in range(HALVES):
            if t > 0:
                right_copy(t - 1, h).wait_recv()
            if t < n_right:
                right_copy(t, h).start()
            if t > 0:
                pair_copy(t, from_right_going(t), h).start()
            if t == 0:
                pair_copy(0, y, h).start()
            if 0 < t <= n_left:
                left_copy(t - 1, h).wait_recv()
            if t < n_left:
                left_copy(t, h).start()
            if 0 < t <= n_left:
                pair_copy(n_right + t, from_left_going(t), h).start()

    gather_step(0)

    def exchange(k):
        dest = lax.rem(dp + k, n_dp)
        return pltpu.make_async_remote_copy(
            stage_src.at[dest],
            stage_dst.at[dp],
            a2a_send.at[k],
            a2a_recv.at[k],
            at_dp(dest),
            MESH,
        )

    keep = pltpu.make_async_copy(stage_src.at[dp], stage_dst.at[dp], a2a_recv.at[0])
    keep.start()

    def exchange_start(k, carry):
        exchange(k).start()
        return carry

    lax.fori_loop(1, n_dp, exchange_start, 0)

    def top_copy():
        return pltpu.make_async_remote_copy(
            top_ref,
            g_in.at[PIPE - 1 - pos],
            top_send,
            g_recv.at[PIPE - 1 - pos],
            at_pos(PIPE - 1),
            MESH,
        )

    @pl.when(pos == PIPE - 1)
    def _():
        pltpu.make_async_copy(top_ref, g_in.at[0], g_recv.at[0]).start()

    @pl.when(pos != PIPE - 1)
    def _():
        top_copy().start()

    def exchange_wait(k, carry):
        exchange(k).wait_recv()
        return carry

    lax.fori_loop(1, n_dp, exchange_wait, 0)
    keep.wait()
    image[0:half_rows, :] = stage_dst[:, 0, 0:width].astype(BF16)
    image[half_rows : 2 * half_rows, :] = stage_dst[:, 0, width : 2 * width].astype(BF16)

    def feed_copy():
        return pltpu.make_async_remote_copy(
            image, x_in.at[pos], feed_send, x_recv.at[pos], at_pos(0), MESH
        )

    @pl.when(pos == 0)
    def _():
        pltpu.make_async_copy(image, x_in.at[0], x_recv.at[0]).start()

    @pl.when(pos != 0)
    def _():
        feed_copy().start()

    for t in range(1, n_right + 1):
        gather_step(t)
    own_copy.wait()
    for i in range(ny):
        for h in range(HALVES):
            pair_copy(i, y, h).wait_recv()

    span = width // HALVES

    def x_copy(m, h):
        cols = pl.ds(h * span, span)
        return pltpu.make_async_remote_copy(
            x_out.at[m, :, cols],
            x_in.at[m, :, cols],
            x_send.at[m],
            x_recv.at[m],
            at_pos(lax.rem(pos + 1, PIPE)),
            MESH,
        )

    def x_whole(m):
        return pltpu.make_async_remote_copy(
            x_out.at[m], x_in.at[m], x_send.at[m], x_recv.at[m], at_pos(lax.rem(pos + 1, PIPE)), MESH
        )

    def g_copy(m):
        return pltpu.make_async_remote_copy(
            g_out.at[m],
            g_in.at[m],
            g_send.at[m],
            g_recv.at[m],
            at_pos(lax.rem(pos + PIPE - 1, PIPE)),
            MESH,
        )

    depth = image.shape[0]

    def band(m):
        return pl.ds(pl.multiple_of(m * depth, depth), depth)

    def forward(m):
        x_whole(m).wait_recv()
        x = x_in[m].astype(F32)
        r = lax.rsqrt(jnp.mean(x * x, axis=1, keepdims=True) + EPS)
        u = x * r
        mask = maskw[m][:, 0:1]
        q = 1.0 + jnp.sum(u * mask, axis=0, keepdims=True)
        h = (u * q).astype(BF16)
        u_s[m] = u
        r_s[m] = jnp.broadcast_to(r, (depth, 128))
        q_s[m] = q
        hid[band(m), :] = h
        for half in range(HALVES):
            cols = slice(half * span, (half + 1) * span)
            pre = dot(h, wfull[:, cols])
            gate = 0.5 * jnp.tanh(0.5 * pre) + 0.5
            slope_s[m, :, cols] = gate * (1.0 + pre * (1.0 - gate))

            @pl.when(pos < PIPE - 1)
            def _():
                x_out[m, :, cols] = (x[:, cols] + pre * gate).astype(BF16)
                x_copy(m, half).start()

    def backward(m):
        g_copy(m).wait_recv()
        g = g_in[m].astype(F32)
        slope = (g * slope_s[m]).astype(BF16)
        slp[band(m), :] = slope

        @pl.when(pos > 0)
        def _():
            b = dot(slope, wfull[...], 1, 1)
            u = u_s[m]
            mask = maskw[m][:, 0:1]
            r = r_s[m][:, 0:1]
            du = b * q_s[m] + mask * jnp.sum(b * u, axis=0, keepdims=True)
            mean = jnp.mean(du * u, axis=1, keepdims=True)
            g_out[m] = (g + r * (du - u * mean)).astype(BF16)
            g_copy(m).start()

    lag = jnp.where(pos == PIPE - 1, 0, jnp.where(pos == PIPE - 2, 5, PIPE))

    def turn(t, carry):
        @pl.when(t < PIPE)
        def _():
            forward(t)

        @pl.when((t >= lag) & (t < lag + PIPE))
        def _():
            backward(t - lag)

        return carry

    lax.fori_loop(0, 2 * PIPE, turn, 0)

    def target(i):
        if i == ny - 1:
            return y
        if i % 2 == 0:
            return lax.rem(y + n_right - i // 2, ny)
        return lax.rem(y + ny - n_left + i // 2, ny)

    def pr_copy(i):
        return pltpu.make_async_remote_copy(
            pair_src.at[i], pair_dst.at[i], pr_send.at[i], pr_recv.at[i], at_dp(partner), MESH
        )

    def mine(i, h):
        base = pl.multiple_of(target(i) * 2 * rows + c * rows + h * sub, sub)
        return dw[pl.ds(base, sub), :] + pair_dst[i, h * sub : (h + 1) * sub, :].astype(F32)

    for i in range(ny):
        block = target(i)
        at = pl.multiple_of(block * 2 * rows, 2 * rows)
        dw[pl.ds(at, 2 * rows), :] = dot(hid[:, pl.ds(at, 2 * rows)], slp[...], 0, 0)
        theirs = pl.multiple_of(block * 2 * rows + (1 - c) * rows, rows)
        pair_src[i] = dw[pl.ds(theirs, rows), :].astype(BF16)
        pr_copy(i).start()

    def rr_copy(t, h):
        part = pl.ds(h * sub, sub)
        return pltpu.make_async_remote_copy(
            ring_src.at[2 * t, part],
            ring_dst.at[2 * t, part],
            rr_send.at[t, h],
            rr_recv.at[t, h],
            at_dp(up),
            MESH,
        )

    def rl_copy(t, h):
        part = pl.ds(h * sub, sub)
        return pltpu.make_async_remote_copy(
            ring_src.at[2 * t + 1, part],
            ring_dst.at[2 * t + 1, part],
            rl_send.at[t, h],
            rl_recv.at[t, h],
            at_dp(down),
            MESH,
        )

    def arrived(slot, h):
        return ring_dst[slot, h * sub : (h + 1) * sub, :].astype(F32)

    for t in range(n_right):
        pr_copy(2 * t).wait_recv()
        if t < n_left:
            pr_copy(2 * t + 1).wait_recv()
        for h in range(HALVES):
            total = mine(2 * t, h)
            if t > 0:
                rr_copy(t - 1, h).wait_recv()
                total = total + arrived(2 * (t - 1), h)
            ring_src[2 * t, h * sub : (h + 1) * sub, :] = total.astype(BF16)
            rr_copy(t, h).start()
            if t < n_left:
                total = mine(2 * t + 1, h)
                if t > 0:
                    rl_copy(t - 1, h).wait_recv()
                    total = total + arrived(2 * (t - 1) + 1, h)
                ring_src[2 * t + 1, h * sub : (h + 1) * sub, :] = total.astype(BF16)
                rl_copy(t, h).start()
    pr_copy(ny - 1).wait_recv()
    for h in range(HALVES):
        total = mine(ny - 1, h)
        rl_copy(n_left - 1, h).wait_recv()
        total = total + arrived(2 * (n_left - 1) + 1, h)
        rr_copy(n_right - 1, h).wait_recv()
        total = total + arrived(2 * (n_right - 1), h)
        out_ref[h * sub : (h + 1) * sub, :] = total

    for h in range(HALVES):
        for t in range(n_right):
            right_copy(t, h).wait_send()
            rr_copy(t, h).wait_send()
        for t in range(n_left):
            left_copy(t, h).wait_send()
            rl_copy(t, h).wait_send()
        for i in range(ny):
            pair_copy(i, y, h).wait_send()
    for i in range(ny):
        pr_copy(i).wait_send()

    def exchange_sent(k, carry):
        exchange(k).wait_send()
        return carry

    lax.fori_loop(1, n_dp, exchange_sent, 0)

    @pl.when(pos != PIPE - 1)
    def _():
        top_copy().wait_send()

        def sent(m, carry):
            x_whole(m).wait_send()
            return carry

        lax.fori_loop(0, PIPE, sent, 0)

    @pl.when(pos != 0)
    def _():
        feed_copy().wait_send()

        def sent(m, carry):
            g_copy(m).wait_send()
            return carry

        lax.fori_loop(0, PIPE, sent, 0)


def local(n_dp, lat_raw, txt_raw, lat_embed, txt_embed, image_owner, text_len, weights, top_grad):
    lat = lat_raw.reshape(lat_raw.shape[1], lat_raw.shape[3])
    txt = txt_raw.reshape(txt_raw.shape[1], txt_raw.shape[3])
    w = weights[0]
    top = top_grad[0, 0]
    rows, width = w.shape
    depth = top.shape[0]
    ny = n_dp // 2
    n_right = ny // 2
    n_left = ny - 1 - n_right
    vmem = pl.BlockSpec(memory_space=pltpu.VMEM)
    dma = pltpu.SemaphoreType.DMA
    out = pl.pallas_call(
        functools.partial(kernel, n_dp),
        out_shape=jax.ShapeDtypeStruct((rows, width), F32),
        in_specs=[
            vmem,
            vmem,
            vmem,
            pl.BlockSpec(memory_space=pl.ANY),
            vmem,
            vmem,
            vmem,
            vmem,
        ],
        out_specs=vmem,
        scratch_shapes=[
            pltpu.VMEM(txt_embed.shape, BF16),
            pltpu.VMEM((width, width), BF16),
            pltpu.VMEM((n_dp, 1, 2 * width), F32),
            pltpu.VMEM((n_dp, 1, 2 * width), F32),
            pltpu.VMEM((depth, width), BF16),
            pltpu.VMEM((PIPE, depth, 128), F32),
            pltpu.VMEM((PIPE, depth, width), BF16),
            pltpu.VMEM((PIPE, depth, width), BF16),
            pltpu.VMEM((PIPE, depth, width), BF16),
            pltpu.VMEM((PIPE, depth, width), BF16),
            pltpu.VMEM((PIPE * depth, width), BF16),
            pltpu.VMEM((PIPE * depth, width), BF16),
            pltpu.VMEM((PIPE, depth, width), F32),
            pltpu.VMEM((PIPE, depth, width), F32),
            pltpu.VMEM((PIPE, depth, 128), F32),
            pltpu.VMEM((PIPE, 1, width), F32),
            pltpu.VMEM((width, width), F32),
            pltpu.VMEM((ny, rows, width), BF16),
            pltpu.VMEM((ny, rows, width), BF16),
            pltpu.VMEM((ny - 1, rows, width), BF16),
            pltpu.VMEM((ny - 1, rows, width), BF16),
            dma((CHUNKS,)),
            dma,
            dma((n_right, HALVES)),
            dma((n_right, HALVES)),
            dma((n_left, HALVES)),
            dma((n_left, HALVES)),
            dma((ny, HALVES)),
            dma((ny, HALVES)),
            dma((n_dp,)),
            dma((n_dp,)),
            dma((PIPE,)),
            dma((PIPE,)),
            dma((PIPE,)),
            dma((PIPE,)),
            dma,
            dma,
            dma((ny,)),
            dma((ny,)),
            dma((n_right, HALVES)),
            dma((n_right, HALVES)),
            dma((n_left, HALVES)),
            dma((n_left, HALVES)),
        ],
        compiler_params=pltpu.CompilerParams(
            collective_id=0, has_side_effects=True, vmem_limit_bytes=56 * 1024 * 1024
        ),
        name="cascade",
    )(lat, txt, lat_embed, txt_embed, image_owner.T, text_len.T, w, top)
    return out[None]


def solution(mesh):
    placed = (
        P("section", None, "dp", None),
        P("section", None, "dp", None),
        P(),
        P(),
        P(),
        P(),
        P("section", "dp", None),
        P("dp", "section", None, None),
    )
    return jax.shard_map(
        functools.partial(local, mesh.shape["dp"]),
        mesh=mesh,
        in_specs=placed,
        out_specs=P("section", "dp", None),
        check_vma=False,
    )
```

time: 697 us -> 130 us (0.19)
  the two profiles are of different devices: /device:TPU:27 before, /device:TPU:8 now
where the time goes in v1:
time: 130 us
  Pallas kernels  129 us (99%)
  local copies, waits for them, and re-layouts  1.67 us (1%)
    pallas_call x1, Pallas kernels, local(): pl.pallas_call(functools.partial(kernel, n_dp), out_shape=jax.ShapeDtypeS...  129 us

profile of v1, /device:TPU:8, one launch (start us, length us, event | category | flops | bytes accessed | tf_op | source)
XLA Modules:
  0.0 130.3 jit_solution(4868032532478126986)
XLA Ops:
  0.0 128.6 %cascade.1 = f32[64,1024]{1,0:T(8,128)} custom-call(bf16[16,16]{1,0:T(8,128)(2,1)} %bitcast.13, bf16[16,4096]{1,0:T(8,128)(2,1)} %bitcast.8, bf16[16,1024]{1,0:T(8,128)(2,1)} %late_ref.1, bf16[4096,1024]{1,0:T(8,128)(2,1)} %txte_ref.1, s32[16,48]{1,0:T(8,128)} %bitcast.11, s32[16,48]{1,0:T(8,128)} %bitcast.12, bf16[64,1024]{1,0:T(8,128)(2,1)} %bitcast.9, ...), custom_call_target="tpu_custom_call" | custom-call | tf_op jit(solution)/shard_map/cascade/pallas_call | solution.py:499
  128.6 1.7 %copy.10 = f32[1,64,1024]{2,1,0:T(8,128)} copy(f32[1,64,1024]{2,1,0:T(8,128)} %bitcast.7) | data formatting | bytes 524288
